TPU v7x, 32 devices: a whole 2x2x4 slice. The times are simulated.
32 devices in a mesh: blk: 8 (over z, y), lblk: 4 (over x, core).
Axes of the slice: x: 2, y: 2, z: 4, core: 2. Of those that a mesh axis runs over, the one named last changes fastest.
Arguments:
- sky: bfloat16 [8, 2, 32, 16384], P(None, None, 'blk', 'lblk'), may hold values from -6 to 6
- arc_start: int32 [2, 32], P(None, 'blk'), may hold values from 0 to 16383
- arc_count: int32 [2, 32], P(None, 'blk'), may hold values from 4096 to 16384
- owner_modes: int32 [32], replicated, may hold values from 0 to 31, each once
- legendre: bfloat16 [32, 8, 4, 4096], P('blk', None, None, 'lblk'), may hold values from -1 to 1
Outputs:
- alm: float32 [8, 2, 32, 4096], P(None, None, 'blk', 'lblk')
Inputs may be any that keep to these rules, and one draw needn't show every extreme that they name: `owner_modes`: each m-mode 0 to 31 appears exactly once.
All inputs are finite; a program needn't handle non-finite values.
Results may differ from a plain program's by a relative error of at most 0.0049.
Values may be sent and summed in bfloat16 or wider, within the bound.
No kernel may reach another device: no remote copies, remote signals or barrier semaphores. Data moves between devices by JAX's collectives and lax.ppermute only.
A program may use at most 64 MiB of HBM per device.

v0:
```python
import math
import jax
import jax.numpy as jnp
from jax import lax
from jax.sharding import PartitionSpec as P

RLEN = 16384
DIFFUSION = 0.2


def padded(x, sides, width, wrap):
    for axis, dim in sides:
        count, length = (lax.axis_size(axis), x.shape[dim])
        up = [(i, (i + 1) % count) for i in range(count if wrap else count - 1)]
        down = [(j, i) for i, j in up]
        last = lax.slice_in_dim(x, length - width, length, axis=dim)
        initial = lax.slice_in_dim(x, 0, width, axis=dim)
        before = lax.ppermute(last, axis, up)
        after = lax.ppermute(initial, axis, down)
        x = jnp.concatenate([before, x, after], axis=dim)
    return x


def mode_basis(positions, mode_list):
    product_index = jnp.mod(positions[:, None] * mode_list[None, :], RLEN)
    angles = 2.0 * math.pi / RLEN * product_index.astype(jnp.float32)
    return (jnp.cos(angles).astype(jnp.bfloat16), (-jnp.sin(angles)).astype(jnp.bfloat16))


def legendre_section(fourier, legendre_rows, my_modes, degrees):
    north_part = fourier[:, 0].astype(jnp.float32)
    south_part = fourier[:, 1].astype(jnp.float32)
    folded = jnp.concatenate([north_part + south_part, north_part - south_part], axis=2).astype(
        jnp.bfloat16
    )
    latitude_sums = jnp.einsum(
        "xrys,srl->xysl", folded, legendre_rows, preferred_element_type=jnp.float32
    )
    even_parity = jnp.mod(degrees[None, :] + my_modes[:, None], 2) == 0
    chosen = jnp.where(even_parity[None, None], latitude_sums[:, :2], latitude_sums[:, 2:])
    inside = (degrees[None, :] >= my_modes[:, None])[None, None]
    return jnp.where(inside, chosen, jnp.zeros((), jnp.float32))


def local(sky, arc_start, arc_count, owner_modes, legendre):
    maps_here = sky.shape[0]
    band_here = sky.shape[2]
    quarter = sky.shape[3]
    column = lax.axis_index("lblk")
    positions = column * quarter + jnp.arange(quarter, dtype=jnp.int32)
    offset = jnp.mod(positions[None, None, :] - arc_start[:, :, None], RLEN)
    kept_mask = offset < arc_count[:, :, None]
    masked = jnp.where(kept_mask[None], sky, jnp.zeros((), jnp.bfloat16))
    layered = padded(masked, (("blk", 2),), 1, False)
    edge_padded = padded(masked, (("lblk", 3),), 1, True)
    is_last = lax.axis_index("blk") == lax.axis_size("blk") - 1
    beyond = jnp.where(is_last, masked[:, ::-1, band_here - 1 :], layered[:, :, band_here + 1 :])
    centre = masked.astype(jnp.float32)
    layer_above = layered[:, :, :band_here].astype(jnp.float32)
    layer_below = jnp.concatenate([layered[:, :, 2 : band_here + 1], beyond], axis=2).astype(
        jnp.float32
    )
    pixel_before = edge_padded[:, :, :, :quarter].astype(jnp.float32)
    pixel_after = edge_padded[:, :, :, 2:].astype(jnp.float32)
    total = layer_above + layer_below + pixel_before + pixel_after - 4.0 * centre
    smooth = (centre + DIFFUSION * total).astype(jnp.bfloat16)
    cos_table, sin_table = mode_basis(positions, owner_modes)
    slab_size = owner_modes.shape[0]
    flat_rows = smooth.reshape(maps_here * 2 * band_here, quarter)
    real_part = jnp.dot(flat_rows, cos_table, preferred_element_type=jnp.float32).reshape(
        maps_here, 2, band_here, slab_size
    )
    imag_part = jnp.dot(flat_rows, sin_table, preferred_element_type=jnp.float32).reshape(
        maps_here, 2, band_here, slab_size
    )
    parity = jnp.arange(band_here, dtype=jnp.int32) % 2
    phase_turn = math.pi / RLEN * (parity[:, None] * owner_modes[None, :]).astype(jnp.float32)
    turn_cos = jnp.cos(phase_turn)
    turn_sin = jnp.sin(phase_turn)
    norm_scale = 1.0 / math.sqrt(RLEN)
    rotated_real = (real_part * turn_cos + imag_part * turn_sin) * norm_scale
    rotated_imag = (imag_part * turn_cos - real_part * turn_sin) * norm_scale
    partial_value = jnp.stack([rotated_real, rotated_imag], axis=3)
    owned_count = legendre.shape[0]
    degree_part = legendre.shape[3]
    my_modes = lax.dynamic_slice_in_dim(
        owner_modes, lax.axis_index("blk") * owned_count, owned_count
    )
    degrees = column * degree_part + jnp.arange(degree_part, dtype=jnp.int32)
    legendre_rows = legendre.reshape(owned_count, -1, degree_part)
    spread = lax.all_to_all(partial_value, "blk", split_axis=4, concat_axis=2, tiled=True)
    summed = lax.psum(spread, "lblk")
    fourier = summed.astype(jnp.bfloat16)
    result = legendre_section(fourier, legendre_rows, my_modes, degrees)
    return result


def solution(mesh):
    return jax.shard_map(
        local,
        mesh=mesh,
        in_specs=(
            P(None, None, "blk", "lblk"),
            P(None, "blk"),
            P(None, "blk"),
            P(),
            P("blk", None, None, "lblk"),
        ),
        out_specs=P(None, None, "blk", "lblk"),
        check_vma=False,
    )
```

profile of v0, /device:TPU:0, one launch (start us, length us, event | category | flops | bytes accessed | tf_op | source)
XLA Modules:
  0.0 53.8 jit_solution(13409327666316147105)
XLA Ops:
  0.0 0.0 copy-start.1
  0.0 0.0 copy-start.2
  0.0 0.7 %copy-done.1 = s32[2,4]{1,0:T(2,128)S(1)} copy-done((s32[2,4]{1,0:T(2,128)S(1)}, s32[2,4]{1,0:T(2,128)}, u32[]{:S(2)}) %copy-start.1) | copy-done | bytes 56
  0.7 0.0 copy-done.2
  0.7 0.2 fusion.16
  0.9 1.3 %broadcast_select_fusion.1 = bf16[8,2,4,4096]{3,2,1,0:T(4,128)(2,1)S(1)} fusion(bf16[8,2,4,4096]{3,2,1,0:T(4,128)(2,1)} %param.5, pred[2,4,4096]{2,1,0:T(4,128)(4,1)S(1)} %fusion.16), kind=kLoop, calls=%fused_computation.20 | loop fusion | flops 262144 | bytes 1081344 | tf_op jit(solution)/shard_map/jit(_where)/select_n | solution.py:53
  2.2 0.6 %fusion.38 = (bf16[8,2,1,4096]{3,2,1,0:T(2,128)(2,1)S(1)}, bf16[8,2,1,4096]{3,2,1,0:T(2,128)(2,1)S(1)}) fusion(bf16[8,2,4,4096]{3,2,1,0:T(4,128)(2,1)S(1)} %broadcast_select_fusion.1), kind=kLoop, calls=%fused_computation.70 | loop fusion | bytes 524288 | tf_op jit(solution)/shard_map/slice | solution.py:17
  2.8 1.3 %collective-permute-start.1 = (bf16[8,2,1,4096]{3,2,1,0:T(2,128)(2,1)S(1)}, bf16[8,2,1,4096]{3,2,1,0:T(2,128)(2,1)S(1)}, u32[]{:S(2)}, u32[]{:S(2)}) collective-permute-start(bf16[8,2,1,4096]{3,2,1,0:T(2,128)(2,1)S(1)} %get-tuple-element.5), channel_id=1, source_target_pairs={{4,0},{8,4},{12,8},{16,12},{20,16},{24,20},{28,24},{5,1},{9,5},{13... | collective-permute-start | bytes 393224 | tf_op jit(solution)/shard_map/ppermute | solution.py:19
  4.1 5.5 %collective-permute-start = (bf16[8,2,1,4096]{3,2,1,0:T(2,128)(2,1)S(1)}, bf16[8,2,1,4096]{3,2,1,0:T(2,128)(2,1)S(1)}, u32[]{:S(2)}, u32[]{:S(2)}) collective-permute-start(bf16[8,2,1,4096]{3,2,1,0:T(2,128)(2,1)S(1)} %get-tuple-element.6), channel_id=1, source_target_pairs={{0,4},{4,8},{8,12},{12,16},{16,20},{20,24},{24,28},{1,5},{5,9},{9,... | collective-permute-start | bytes 393224 | tf_op jit(solution)/shard_map/ppermute | solution.py:18
  9.6 0.1 fusion.39
  9.7 0.1 collective-permute-start.2
  9.8 0.0 copy-start.3
  9.8 1.7 %collective-permute-start.3 = (bf16[8,2,4,1]{3,2,1,0:T(4,128)(2,1)S(1)}, bf16[8,2,4,1]{3,2,1,0:T(4,128)(2,1)S(1)}, u32[]{:S(2)}, u32[]{:S(2)}) collective-permute-start(bf16[8,2,4,1]{3,2,1,0:T(4,128)(2,1)S(1)} %get-tuple-element.8), channel_id=1, source_target_pairs={{1,0},{2,1},{3,2},{0,3},{5,4},{6,5},{7,6},{4,7},{9,8},{10,9},{11,1... | collective-permute-start | bytes 392 | tf_op jit(solution)/shard_map/ppermute | solution.py:19
  11.5 0.0 copy-done.3
  11.5 0.1 fusion.28
  11.6 0.3 slice.52
  11.9 0.1 dynamic_slice.3
  12.0 2.0 %collective-permute-done.1 = bf16[8,2,1,4096]{3,2,1,0:T(2,128)(2,1)S(1)} collective-permute-done((bf16[8,2,1,4096]{3,2,1,0:T(2,128)(2,1)S(1)}, bf16[8,2,1,4096]{3,2,1,0:T(2,128)(2,1)S(1)}, u32[]{:S(2)}, u32[]{:S(2)}) %collective-permute-start.1) | collective-permute-done | bytes 131104 | tf_op jit(solution)/shard_map/ppermute | solution.py:19
  14.0 0.4 broadcast_select_fusion
  14.4 0.0 collective-permute-done.2
  14.4 0.0 collective-permute-done.3
  14.4 5.3 %collective-permute-done = bf16[8,2,1,4096]{3,2,1,0:T(2,128)(2,1)S(1)} collective-permute-done((bf16[8,2,1,4096]{3,2,1,0:T(2,128)(2,1)S(1)}, bf16[8,2,1,4096]{3,2,1,0:T(2,128)(2,1)S(1)}, u32[]{:S(2)}, u32[]{:S(2)}) %collective-permute-start) | collective-permute-done | bytes 131104 | tf_op jit(solution)/shard_map/ppermute | solution.py:18
  19.7 2.3 %fusion.2 = bf16[8,2,4,4096]{3,2,1,0:T(4,128)(2,1)S(1)} fusion(bf16[8,2,4,4096]{3,2,1,0:T(4,128)(2,1)S(1)} %broadcast_select_fusion.1, bf16[8,2,4,1]{3,2,1,0:T(4,128)(2,1)S(1)} %collective-permute-done.3, bf16[8,2,4,1]{3,2,1,0:T(4,128)(2,1)S(1)} %collective-permute-done.2, bf16[8,2,1,4096]{3,2,1,0:T(2,128)(2,1)S(1)} %collective-permute-done, ...), kind=kLoop, calls=%fused_computation.5 | loop fusion | flops 6553600 | bytes 1704192 | tf_op jit(solution)/shard_map/convert_element_type | solution.py:66
  22.0 2.2 %fusion.7 = f32[8,2,4,32]{3,2,1,0:T(4,128)S(1)} fusion(bf16[8,2,4,4096]{3,2,1,0:T(4,128)(2,1)S(1)} %fusion.2, s32[32]{0:T(128)S(1)} %copy-done.3, s32[4096]{0:T(1024)S(1)} %iota_add_fusion), kind=kOutput, calls=%fused_computation.22 | convolution fusion | flops 18743296 | bytes 548992 | tf_op jit(solution)/shard_map/dot_general | solution.py:70
  24.3 2.3 %multiply_bitcast_fusion.1 = (f32[8,2,4,1,32]{4,2,1,0,3:T(4,128)S(1)}, f32[8,2,4,1,32]{4,2,1,0,3:T(4,128)S(1)}) fusion(f32[8,2,4,32]{3,2,1,0:T(4,128)S(1)} %fusion.7, f32[4,32]{1,0:T(4,128)S(1)} %get-tuple-element.16, f32[4,32]{1,0:T(4,128)S(1)} %get-tuple-element.15, bf16[8,2,4,4096]{3,2,1,0:T(4,128)(2,1)S(1)} %fusion.2, s32[32]{0:T(128)S(1)} %copy-done.3, ...), kind=kOutput, calls=%fused_computation.44 | convolution fusion | flops 18890752 | bytes 566400 | tf_op jit(solution)/shard_map/dot_general | solution.py:73
  26.6 0.0 copy-start
  26.6 0.2 copy.16
  26.8 0.9 %reshape.175 = f32[8,1,512]{2,1,0:T(1,128)} reshape(f32[32,2,2,4,8]{4,3,2,1,0:T(4,128)S(1)} %bitcast.33) | data formatting | bytes 32768
  27.7 5.8 %all-to-all-start = ((f32[8,1,512]{2,1,0:T(1,128)}), f32[8,1,512]{2,1,0:T(1,128)S(1)}, u32[]{:S(2)}, u32[]{:S(2)}) async-start(f32[8,1,512]{2,1,0:T(1,128)} %reshape.175), calls=%async_computation | async-start | bytes 32768 | tf_op jit(solution)/shard_map/all_to_all | solution.py:91
  33.5 0.1 broadcast_compare_fusion
  33.6 0.0 copy-done
  33.6 0.1 reshape.173
  33.6 6.4 %all-to-all-done = f32[8,1,512]{2,1,0:T(1,128)S(1)} async-done(((f32[8,1,512]{2,1,0:T(1,128)}), f32[8,1,512]{2,1,0:T(1,128)S(1)}, u32[]{:S(2)}, u32[]{:S(2)}) %all-to-all-start) | async-done | bytes 16416 | tf_op jit(solution)/shard_map/all_to_all | solution.py:91
  40.0 0.5 broadcast.207
  40.5 0.7 %reduce = f32[8,512]{1,0:T(8,128)S(1)} reduce(f32[8,1,512]{2,1,0:T(1,128)S(1)} %all-to-all-done, f32[]{:T(128)} %broadcast.207), dimensions={1}, to_apply=%all_to_all.13.reduce_sub_computation | reduce | bytes 32772 | tf_op jit(solution)/shard_map/all_to_all | solution.py:91
  41.2 0.3 reshape.176
  41.6 0.1 copy.17
  41.7 0.2 copy.18
  41.9 0.1 copy.19
  42.0 10.7 %psum.7 = bf16[8,2,32,2,4]{2,0,3,4,1:T(8,128)(2,1)S(1)} all-reduce(f32[8,2,32,2,4]{2,0,3,4,1:T(8,128)S(1)} %copy.19), channel_id=1, replica_groups=mesh['blk'=8,'lblk'=4] {'lblk'}, use_global_device_ids=true, to_apply=%region_0.1 | all-reduce | flops 4096 | bytes 24576 | tf_op jit(solution)/shard_map/psum | solution.py:92
  52.7 0.2 convolution_bitcast_fusion
  52.9 0.1 fusion.12
  52.9 0.9 %copy.20 = f32[8,2,4,1024]{3,2,1,0:T(4,128)} copy(f32[8,2,4,1024]{3,0,1,2:T(8,128)S(1)} %fusion.12) | data formatting | bytes 524288 | tf_op jit(solution)/shard_map/jit(_where)/select_n | solution.py:42
  (5 shorter events, 0.0 us)
Async XLA Ops:
  0.0 0.7 %copy-start.1 = (s32[2,4]{1,0:T(2,128)S(1)}, s32[2,4]{1,0:T(2,128)}, u32[]{:S(2)}) copy-start(s32[2,4]{1,0:T(2,128)} %param.7) | copy-start | bytes 100
  0.0 0.7 %copy-start.2 = (s32[2,4]{1,0:T(2,128)S(1)}, s32[2,4]{1,0:T(2,128)}, u32[]{:S(2)}) copy-start(s32[2,4]{1,0:T(2,128)} %param.6) | copy-start | bytes 100
  2.8 11.2 %collective-permute-start.1 = (bf16[8,2,1,4096]{3,2,1,0:T(2,128)(2,1)S(1)}, bf16[8,2,1,4096]{3,2,1,0:T(2,128)(2,1)S(1)}, u32[]{:S(2)}, u32[]{:S(2)}) collective-permute-start(bf16[8,2,1,4096]{3,2,1,0:T(2,128)(2,1)S(1)} %get-tuple-element.5), channel_id=1, source_target_pairs={{4,0},{8,4},{12,8},{16,12},{20,16},{24,20},{28,24},{5,1},{9,5},{13... | collective-permute-start | bytes 393224 | tf_op jit(solution)/shard_map/ppermute | solution.py:19
  4.1 15.7 %collective-permute-start = (bf16[8,2,1,4096]{3,2,1,0:T(2,128)(2,1)S(1)}, bf16[8,2,1,4096]{3,2,1,0:T(2,128)(2,1)S(1)}, u32[]{:S(2)}, u32[]{:S(2)}) collective-permute-start(bf16[8,2,1,4096]{3,2,1,0:T(2,128)(2,1)S(1)} %get-tuple-element.6), channel_id=1, source_target_pairs={{0,4},{4,8},{8,12},{12,16},{16,20},{20,24},{24,28},{1,5},{5,9},{9,... | collective-permute-start | bytes 393224 | tf_op jit(solution)/shard_map/ppermute | solution.py:18
  9.7 4.7 %collective-permute-start.2 = (bf16[8,2,4,1]{3,2,1,0:T(4,128)(2,1)S(1)}, bf16[8,2,4,1]{3,2,1,0:T(4,128)(2,1)S(1)}, u32[]{:S(2)}, u32[]{:S(2)}) collective-permute-start(bf16[8,2,4,1]{3,2,1,0:T(4,128)(2,1)S(1)} %get-tuple-element.7), channel_id=1, source_target_pairs={{0,1},{1,2},{2,3},{3,0},{4,5},{5,6},{6,7},{7,4},{8,9},{9,10},{10,1... | collective-permute-start | bytes 392 | tf_op jit(solution)/shard_map/ppermute | solution.py:18
  9.8 1.7 %copy-start.3 = (s32[32]{0:T(128)S(1)}, s32[32]{0:T(128)}, u32[]{:S(2)}) copy-start(s32[32]{0:T(128)} %param.8) | copy-start | bytes 388
  9.8 4.6 %collective-permute-start.3 = (bf16[8,2,4,1]{3,2,1,0:T(4,128)(2,1)S(1)}, bf16[8,2,4,1]{3,2,1,0:T(4,128)(2,1)S(1)}, u32[]{:S(2)}, u32[]{:S(2)}) collective-permute-start(bf16[8,2,4,1]{3,2,1,0:T(4,128)(2,1)S(1)} %get-tuple-element.8), channel_id=1, source_target_pairs={{1,0},{2,1},{3,2},{0,3},{5,4},{6,5},{7,6},{4,7},{9,8},{10,9},{11,1... | collective-permute-start | bytes 392 | tf_op jit(solution)/shard_map/ppermute | solution.py:19
  26.6 7.0 %copy-start = (bf16[4,8,4,1024]{3,2,1,0:T(4,128)(2,1)S(1)}, bf16[4,8,4,1024]{3,2,1,0:T(4,128)(2,1)}, u32[]{:S(2)}) copy-start(bf16[4,8,4,1024]{3,2,1,0:T(4,128)(2,1)} %param.9) | copy-start | bytes 786436
  27.7 12.4 %all-to-all-start = ((f32[8,1,512]{2,1,0:T(1,128)}), f32[8,1,512]{2,1,0:T(1,128)S(1)}, u32[]{:S(2)}, u32[]{:S(2)}) async-start(f32[8,1,512]{2,1,0:T(1,128)} %reshape.175), calls=%async_computation | async-start | bytes 32768 | tf_op jit(solution)/shard_map/all_to_all | solution.py:91
where the time goes:
time: 54.1 us; the launch traced here: 53.8 us
  starting transfers between devices  14.4 us (27%)
  waiting for transfers between devices  13.7 us (25%)
  blocking collectives  10.7 us (20%)
  other arithmetic  5.17 us (10%)
  local copies, waits for them, and re-layouts  4.95 us (9%)
  matrix products  4.74 us (9%)
    psum x1, blocking collectives, local(): summed = lax.psum(spread, 'lblk')  10.7 us
    all_to_all x1, waiting for transfers between devices, local(): lax.all_to_all(partial_value, 'blk', split_axis=4, concat_axis=2, tiled=T...  6.4 us
    all_to_all x1, starting transfers between devices, local(): lax.all_to_all(partial_value, 'blk', split_axis=4, concat_axis=2, tiled=T...  5.78 us
    ppermute x2, starting transfers between devices, padded(): before = lax.ppermute(last, axis, up)  5.6 us
    ppermute x2, waiting for transfers between devices, padded(): before = lax.ppermute(last, axis, up)  5.33 us
    ppermute x2, starting transfers between devices, padded(): after = lax.ppermute(initial, axis, down)  3.01 us
    dot_general x1, matrix products, local(): jnp.dot(flat_rows, sin_table, preferred_element_type=jnp.float32)  2.29 us
    convert_element_type x1, other arithmetic, local(): smooth = (centre + DIFFUSION * total).astype(jnp.bfloat16)  2.27 us
  transfers between devices with their start and end apart: 5, of which 3 were waited for; matrix products, arithmetic and copies ran while one was open for 2% of the time, Pallas kernels for 0%

commit v1 on v0

--- a/solution.py
+++ b/solution.py
@@ -89,7 +89,9 @@
     degrees = column * degree_part + jnp.arange(degree_part, dtype=jnp.int32)
     legendre_rows = legendre.reshape(owned_count, -1, degree_part)
     spread = lax.all_to_all(partial_value, "blk", split_axis=4, concat_axis=2, tiled=True)
-    summed = lax.psum(spread, "lblk")
+    summed = spread
+    for hop in (1, 2):
+        summed = summed + lax.ppermute(summed, "lblk", [(dev, dev ^ hop) for dev in range(4)])
     fourier = summed.astype(jnp.bfloat16)
     result = legendre_section(fourier, legendre_rows, my_modes, degrees)
     return result

time: 54.1 us -> 49.1 us (0.908)
  blocking collectives: 10.7 us -> 0 us
  waiting for transfers between devices: 13.7 us -> 17 us
  starting transfers between devices: 14.4 us -> 16 us
  local copies, waits for them, and re-layouts: 4.95 us -> 5.58 us
    psum x1 -> x0, blocking collectives: 10.7 us -> none  [local(): summed = lax.psum(spread, 'lblk')]
    ppermute x0 -> x2, waiting for transfers between devices: none -> 3.75 us  [local(): lax.ppermute(summed, 'lblk', [(dev, dev ^ hop) for dev in range(4)])]
    ppermute x0 -> x2, starting transfers between devices: none -> 1.6 us  [local(): lax.ppermute(summed, 'lblk', [(dev, dev ^ hop) for dev in range(4)])]
    unnamed x10, local copies, waits for them, and re-layouts: 1.9 us -> 2.54 us
    ppermute x2, waiting for transfers between devices: 1.95 us -> 1.38 us  [padded(): after = lax.ppermute(initial, axis, down)]
  transfers between devices with their start and end apart: 5 -> 7, of which waited for: 3 -> 5; matrix products, arithmetic and copies ran while one was open for 2% -> 2% of each run, Pallas kernels for 0% -> 0%
where the time goes in v1:
time: 49.1 us; the launch traced here: 48.8 us
  waiting for transfers between devices  17 us (35%)
  starting transfers between devices  16 us (33%)
  local copies, waits for them, and re-layouts  5.58 us (11%)
  other arithmetic  5.19 us (11%)
  matrix products  4.74 us (10%)
    all_to_all x1, waiting for transfers between devices, local(): lax.all_to_all(partial_value, 'blk', split_axis=4, concat_axis=2, tiled=T...  6.58 us
    all_to_all x1, starting transfers between devices, local(): lax.all_to_all(partial_value, 'blk', split_axis=4, concat_axis=2, tiled=T...  5.78 us
    ppermute x2, starting transfers between devices, padded(): before = lax.ppermute(last, axis, up)  5.6 us
    ppermute x2, waiting for transfers between devices, padded(): before = lax.ppermute(last, axis, up)  5.33 us
    ppermute x2, waiting for transfers between devices, local(): lax.ppermute(summed, 'lblk', [(dev, dev ^ hop) for dev in range(4)])  3.75 us
    ppermute x2, starting transfers between devices, padded(): after = lax.ppermute(initial, axis, down)  3.02 us
    unnamed x10, local copies, waits for them, and re-layouts  2.54 us
    dot_general x1, matrix products, local(): jnp.dot(flat_rows, sin_table, preferred_element_type=jnp.float32)  2.29 us
  transfers between devices with their start and end apart: 7, of which 5 were waited for; matrix products, arithmetic and copies ran while one was open for 2% of the time, Pallas kernels for 0%

profile of v1, /device:TPU:0, one launch (start us, length us, event | category | flops | bytes accessed | tf_op | source)
XLA Modules:
  0.0 48.8 jit_solution(423914419627697912)
XLA Ops:
  0.0 0.0 copy-start.1
  0.0 0.0 copy-start.2
  0.0 0.7 %copy-done.1 = s32[2,4]{1,0:T(2,128)S(1)} copy-done((s32[2,4]{1,0:T(2,128)S(1)}, s32[2,4]{1,0:T(2,128)}, u32[]{:S(2)}) %copy-start.1) | copy-done | bytes 56
  0.7 0.0 copy-done.2
  0.7 0.2 fusion.16
  0.9 1.3 %broadcast_select_fusion.1 = bf16[8,2,4,4096]{3,2,1,0:T(4,128)(2,1)S(1)} fusion(bf16[8,2,4,4096]{3,2,1,0:T(4,128)(2,1)} %param.5, pred[2,4,4096]{2,1,0:T(4,128)(4,1)S(1)} %fusion.16), kind=kLoop, calls=%fused_computation.20 | loop fusion | flops 262144 | bytes 1081344 | tf_op jit(solution)/shard_map/jit(_where)/select_n | solution.py:53
  2.2 0.6 %fusion.38 = (bf16[8,2,1,4096]{3,2,1,0:T(2,128)(2,1)S(1)}, bf16[8,2,1,4096]{3,2,1,0:T(2,128)(2,1)S(1)}) fusion(bf16[8,2,4,4096]{3,2,1,0:T(4,128)(2,1)S(1)} %broadcast_select_fusion.1), kind=kLoop, calls=%fused_computation.71 | loop fusion | bytes 524288 | tf_op jit(solution)/shard_map/slice | solution.py:17
  2.8 1.3 %collective-permute-start.1 = (bf16[8,2,1,4096]{3,2,1,0:T(2,128)(2,1)S(1)}, bf16[8,2,1,4096]{3,2,1,0:T(2,128)(2,1)S(1)}, u32[]{:S(2)}, u32[]{:S(2)}) collective-permute-start(bf16[8,2,1,4096]{3,2,1,0:T(2,128)(2,1)S(1)} %get-tuple-element.5), channel_id=1, source_target_pairs={{4,0},{8,4},{12,8},{16,12},{20,16},{24,20},{28,24},{5,1},{9,5},{13... | collective-permute-start | bytes 393224 | tf_op jit(solution)/shard_map/ppermute | solution.py:19
  4.1 5.5 %collective-permute-start = (bf16[8,2,1,4096]{3,2,1,0:T(2,128)(2,1)S(1)}, bf16[8,2,1,4096]{3,2,1,0:T(2,128)(2,1)S(1)}, u32[]{:S(2)}, u32[]{:S(2)}) collective-permute-start(bf16[8,2,1,4096]{3,2,1,0:T(2,128)(2,1)S(1)} %get-tuple-element.6), channel_id=1, source_target_pairs={{0,4},{4,8},{8,12},{12,16},{16,20},{20,24},{24,28},{1,5},{5,9},{9,... | collective-permute-start | bytes 393224 | tf_op jit(solution)/shard_map/ppermute | solution.py:18
  9.6 0.1 fusion.39
  9.7 0.1 collective-permute-start.2
  9.8 1.7 %collective-permute-start.3 = (bf16[8,2,4,1]{3,2,1,0:T(4,128)(2,1)S(1)}, bf16[8,2,4,1]{3,2,1,0:T(4,128)(2,1)S(1)}, u32[]{:S(2)}, u32[]{:S(2)}) collective-permute-start(bf16[8,2,4,1]{3,2,1,0:T(4,128)(2,1)S(1)} %get-tuple-element.8), channel_id=1, source_target_pairs={{1,0},{2,1},{3,2},{0,3},{5,4},{6,5},{7,6},{4,7},{9,8},{10,9},{11,1... | collective-permute-start | bytes 392 | tf_op jit(solution)/shard_map/ppermute | solution.py:19
  11.5 0.3 slice.52
  11.8 0.0 copy-start.3
  11.8 0.6 %copy-done.3 = s32[32]{0:T(128)S(1)} copy-done((s32[32]{0:T(128)S(1)}, s32[32]{0:T(128)}, u32[]{:S(2)}) %copy-start.3) | copy-done | bytes 152
  12.5 0.1 fusion.28
  12.6 1.4 %collective-permute-done.1 = bf16[8,2,1,4096]{3,2,1,0:T(2,128)(2,1)S(1)} collective-permute-done((bf16[8,2,1,4096]{3,2,1,0:T(2,128)(2,1)S(1)}, bf16[8,2,1,4096]{3,2,1,0:T(2,128)(2,1)S(1)}, u32[]{:S(2)}, u32[]{:S(2)}) %collective-permute-start.1) | collective-permute-done | bytes 131104 | tf_op jit(solution)/shard_map/ppermute | solution.py:19
  14.0 0.4 broadcast_select_fusion
  14.4 0.0 collective-permute-done.2
  14.4 0.0 collective-permute-done.3
  14.4 5.3 %collective-permute-done = bf16[8,2,1,4096]{3,2,1,0:T(2,128)(2,1)S(1)} collective-permute-done((bf16[8,2,1,4096]{3,2,1,0:T(2,128)(2,1)S(1)}, bf16[8,2,1,4096]{3,2,1,0:T(2,128)(2,1)S(1)}, u32[]{:S(2)}, u32[]{:S(2)}) %collective-permute-start) | collective-permute-done | bytes 131104 | tf_op jit(solution)/shard_map/ppermute | solution.py:18
  19.7 2.3 %fusion.2 = bf16[8,2,4,4096]{3,2,1,0:T(4,128)(2,1)S(1)} fusion(bf16[8,2,4,4096]{3,2,1,0:T(4,128)(2,1)S(1)} %broadcast_select_fusion.1, bf16[8,2,4,1]{3,2,1,0:T(4,128)(2,1)S(1)} %collective-permute-done.3, bf16[8,2,4,1]{3,2,1,0:T(4,128)(2,1)S(1)} %collective-permute-done.2, bf16[8,2,1,4096]{3,2,1,0:T(2,128)(2,1)S(1)} %collective-permute-done, ...), kind=kLoop, calls=%fused_computation.5 | loop fusion | flops 6553600 | bytes 1704192 | tf_op jit(solution)/shard_map/convert_element_type | solution.py:66
  22.0 2.2 %fusion.7 = f32[8,2,4,32]{3,2,1,0:T(4,128)S(1)} fusion(bf16[8,2,4,4096]{3,2,1,0:T(4,128)(2,1)S(1)} %fusion.2, s32[32]{0:T(128)S(1)} %copy-done.3, s32[4096]{0:T(1024)S(1)} %iota_add_fusion), kind=kOutput, calls=%fused_computation.22 | convolution fusion | flops 18743296 | bytes 548992 | tf_op jit(solution)/shard_map/dot_general | solution.py:70
  24.3 2.3 %multiply_bitcast_fusion.1 = (f32[8,2,4,1,32]{4,2,1,0,3:T(4,128)S(1)}, f32[8,2,4,1,32]{4,2,1,0,3:T(4,128)S(1)}) fusion(f32[8,2,4,32]{3,2,1,0:T(4,128)S(1)} %fusion.7, f32[4,32]{1,0:T(4,128)S(1)} %get-tuple-element.16, f32[4,32]{1,0:T(4,128)S(1)} %get-tuple-element.15, bf16[8,2,4,4096]{3,2,1,0:T(4,128)(2,1)S(1)} %fusion.2, s32[32]{0:T(128)S(1)} %copy-done.3, ...), kind=kOutput, calls=%fused_computation.45 | convolution fusion | flops 18890752 | bytes 566400 | tf_op jit(solution)/shard_map/dot_general | solution.py:73
  26.6 0.2 copy.17
  26.8 0.9 %reshape.175 = f32[8,1,512]{2,1,0:T(1,128)} reshape(f32[32,2,2,4,8]{4,3,2,1,0:T(4,128)S(1)} %bitcast.33) | data formatting | bytes 32768
  27.7 5.8 %all-to-all-start = ((f32[8,1,512]{2,1,0:T(1,128)}), f32[8,1,512]{2,1,0:T(1,128)S(1)}, u32[]{:S(2)}, u32[]{:S(2)}) async-start(f32[8,1,512]{2,1,0:T(1,128)} %reshape.175), calls=%async_computation | async-start | bytes 32768 | tf_op jit(solution)/shard_map/all_to_all | solution.py:91
  33.4 6.6 %all-to-all-done = f32[8,1,512]{2,1,0:T(1,128)S(1)} async-done(((f32[8,1,512]{2,1,0:T(1,128)}), f32[8,1,512]{2,1,0:T(1,128)S(1)}, u32[]{:S(2)}, u32[]{:S(2)}) %all-to-all-start) | async-done | bytes 16416 | tf_op jit(solution)/shard_map/all_to_all | solution.py:91
  40.0 0.5 %broadcast.207 = f32[]{:T(128)} broadcast(f32[]{:T(128)} %constant.147), dimensions={} | broadcast | bytes 8 | tf_op jit(solution)/shard_map/all_to_all | solution.py:91
  40.5 0.7 %reduce = f32[8,512]{1,0:T(8,128)S(1)} reduce(f32[8,1,512]{2,1,0:T(1,128)S(1)} %all-to-all-done, f32[]{:T(128)} %broadcast.207), dimensions={1}, to_apply=%all_to_all.13.reduce_sub_computation | reduce | bytes 32772 | tf_op jit(solution)/shard_map/all_to_all | solution.py:91
  41.2 0.3 reshape.176
  41.6 0.1 copy.18
  41.7 0.2 copy.19
  41.8 0.0 copy-start
  41.9 0.1 copy.21
  42.0 0.0 collective-permute-start.4
  42.0 0.1 dynamic_slice.3
  42.1 1.1 %collective-permute-done.4 = f32[8,2,32,2,4]{2,0,3,4,1:T(8,128)S(1)} collective-permute-done((f32[8,2,32,2,4]{2,0,3,4,1:T(8,128)S(1)}, f32[8,2,32,2,4]{2,0,3,4,1:T(8,128)S(1)}, u32[]{:S(2)}, u32[]{:S(2)}) %collective-permute-start.4) | collective-permute-done | bytes 16416 | tf_op jit(solution)/shard_map/ppermute | solution.py:94
  43.3 1.6 %collective-permute-start.5 = (f32[8,2,32,2,4]{2,0,3,4,1:T(8,128)S(1)}, f32[8,2,32,2,4]{2,0,3,4,1:T(8,128)S(1)}, u32[]{:S(2)}, u32[]{:S(2)}) collective-permute-start(f32[8,2,32,2,4]{2,0,3,4,1:T(8,128)S(1)} %add.118), channel_id=1, source_target_pairs={{0,2},{1,3},{2,0},{3,1},{4,6},{5,7},{6,4},{7,5},{8,10},{9,11},{10,... | collective-permute-start | bytes 49160 | tf_op jit(solution)/shard_map/ppermute | solution.py:94
  44.8 0.1 broadcast_compare_fusion
  44.9 0.0 copy-done
  44.9 0.1 reshape.173
  45.0 2.6 %collective-permute-done.5 = f32[8,2,32,2,4]{2,0,3,4,1:T(8,128)S(1)} collective-permute-done((f32[8,2,32,2,4]{2,0,3,4,1:T(8,128)S(1)}, f32[8,2,32,2,4]{2,0,3,4,1:T(8,128)S(1)}, u32[]{:S(2)}, u32[]{:S(2)}) %collective-permute-start.5) | collective-permute-done | bytes 16416 | tf_op jit(solution)/shard_map/ppermute | solution.py:94
  47.6 0.2 convolution_bitcast_fusion
  47.9 0.1 fusion.12
  47.9 0.9 %copy.22 = f32[8,2,4,1024]{3,2,1,0:T(4,128)} copy(f32[8,2,4,1024]{3,0,1,2:T(8,128)S(1)} %fusion.12) | data formatting | bytes 524288 | tf_op jit(solution)/shard_map/jit(_where)/select_n | solution.py:42
  (7 shorter events, 0.1 us)
Async XLA Ops:
  0.0 0.7 %copy-start.1 = (s32[2,4]{1,0:T(2,128)S(1)}, s32[2,4]{1,0:T(2,128)}, u32[]{:S(2)}) copy-start(s32[2,4]{1,0:T(2,128)} %param.7) | copy-start | bytes 100
  0.0 0.7 %copy-start.2 = (s32[2,4]{1,0:T(2,128)S(1)}, s32[2,4]{1,0:T(2,128)}, u32[]{:S(2)}) copy-start(s32[2,4]{1,0:T(2,128)} %param.6) | copy-start | bytes 100
  2.8 11.2 %collective-permute-start.1 = (bf16[8,2,1,4096]{3,2,1,0:T(2,128)(2,1)S(1)}, bf16[8,2,1,4096]{3,2,1,0:T(2,128)(2,1)S(1)}, u32[]{:S(2)}, u32[]{:S(2)}) collective-permute-start(bf16[8,2,1,4096]{3,2,1,0:T(2,128)(2,1)S(1)} %get-tuple-element.5), channel_id=1, source_target_pairs={{4,0},{8,4},{12,8},{16,12},{20,16},{24,20},{28,24},{5,1},{9,5},{13... | collective-permute-start | bytes 393224 | tf_op jit(solution)/shard_map/ppermute | solution.py:19
  4.1 15.7 %collective-permute-start = (bf16[8,2,1,4096]{3,2,1,0:T(2,128)(2,1)S(1)}, bf16[8,2,1,4096]{3,2,1,0:T(2,128)(2,1)S(1)}, u32[]{:S(2)}, u32[]{:S(2)}) collective-permute-start(bf16[8,2,1,4096]{3,2,1,0:T(2,128)(2,1)S(1)} %get-tuple-element.6), channel_id=1, source_target_pairs={{0,4},{4,8},{8,12},{12,16},{16,20},{20,24},{24,28},{1,5},{5,9},{9,... | collective-permute-start | bytes 393224 | tf_op jit(solution)/shard_map/ppermute | solution.py:18
  9.7 4.7 %collective-permute-start.2 = (bf16[8,2,4,1]{3,2,1,0:T(4,128)(2,1)S(1)}, bf16[8,2,4,1]{3,2,1,0:T(4,128)(2,1)S(1)}, u32[]{:S(2)}, u32[]{:S(2)}) collective-permute-start(bf16[8,2,4,1]{3,2,1,0:T(4,128)(2,1)S(1)} %get-tuple-element.7), channel_id=1, source_target_pairs={{0,1},{1,2},{2,3},{3,0},{4,5},{5,6},{6,7},{7,4},{8,9},{9,10},{10,1... | collective-permute-start | bytes 392 | tf_op jit(solution)/shard_map/ppermute | solution.py:18
  9.8 4.6 %collective-permute-start.3 = (bf16[8,2,4,1]{3,2,1,0:T(4,128)(2,1)S(1)}, bf16[8,2,4,1]{3,2,1,0:T(4,128)(2,1)S(1)}, u32[]{:S(2)}, u32[]{:S(2)}) collective-permute-start(bf16[8,2,4,1]{3,2,1,0:T(4,128)(2,1)S(1)} %get-tuple-element.8), channel_id=1, source_target_pairs={{1,0},{2,1},{3,2},{0,3},{5,4},{6,5},{7,6},{4,7},{9,8},{10,9},{11,1... | collective-permute-start | bytes 392 | tf_op jit(solution)/shard_map/ppermute | solution.py:19
  11.8 0.7 %copy-start.3 = (s32[32]{0:T(128)S(1)}, s32[32]{0:T(128)}, u32[]{:S(2)}) copy-start(s32[32]{0:T(128)} %param.8) | copy-start | bytes 388
  27.7 12.4 %all-to-all-start = ((f32[8,1,512]{2,1,0:T(1,128)}), f32[8,1,512]{2,1,0:T(1,128)S(1)}, u32[]{:S(2)}, u32[]{:S(2)}) async-start(f32[8,1,512]{2,1,0:T(1,128)} %reshape.175), calls=%async_computation | async-start | bytes 32768 | tf_op jit(solution)/shard_map/all_to_all | solution.py:91
  41.8 3.1 %copy-start = (bf16[4,8,4,1024]{3,2,1,0:T(4,128)(2,1)S(1)}, bf16[4,8,4,1024]{3,2,1,0:T(4,128)(2,1)}, u32[]{:S(2)}) copy-start(bf16[4,8,4,1024]{3,2,1,0:T(4,128)(2,1)} %param.9) | copy-start | bytes 786436
  42.0 1.3 %collective-permute-start.4 = (f32[8,2,32,2,4]{2,0,3,4,1:T(8,128)S(1)}, f32[8,2,32,2,4]{2,0,3,4,1:T(8,128)S(1)}, u32[]{:S(2)}, u32[]{:S(2)}) collective-permute-start(f32[8,2,32,2,4]{2,0,3,4,1:T(8,128)S(1)} %copy.21), channel_id=1, source_target_pairs={{0,1},{1,0},{2,3},{3,2},{4,5},{5,4},{6,7},{7,6},{8,9},{9,8},{10,11... | collective-permute-start | bytes 49160 | tf_op jit(solution)/shard_map/ppermute | solution.py:94
  43.3 4.3 %collective-permute-start.5 = (f32[8,2,32,2,4]{2,0,3,4,1:T(8,128)S(1)}, f32[8,2,32,2,4]{2,0,3,4,1:T(8,128)S(1)}, u32[]{:S(2)}, u32[]{:S(2)}) collective-permute-start(f32[8,2,32,2,4]{2,0,3,4,1:T(8,128)S(1)} %add.118), channel_id=1, source_target_pairs={{0,2},{1,3},{2,0},{3,1},{4,6},{5,7},{6,4},{7,5},{8,10},{9,11},{10,... | collective-permute-start | bytes 49160 | tf_op jit(solution)/shard_map/ppermute | solution.py:94
